TPU v7x, 32 devices: a whole 2x2x4 slice. The times are simulated.
32 devices in a mesh: dp: 4 (over z), ctx: 8 (over y, x, core).
Axes of the slice: x: 2, y: 2, z: 4, core: 2. Of those that a mesh axis runs over, the one named last changes fastest.
Arguments:
- queries: bfloat16 [4, 1024, 1024], P('dp', 'ctx'), may hold values from -6 to 6
- keys: bfloat16 [4, 1024, 1024], P('dp', 'ctx'), may hold values from -6 to 6
- values: bfloat16 [4, 1024, 1024], P('dp', 'ctx'), may hold values from -6 to 6
- outputs: bfloat16 [4, 1024, 1024], P('dp', 'ctx'), may hold values from -1.25 to 1.25
- d_out: bfloat16 [4, 1024, 1024], P('dp', 'ctx'), may hold values from -6 to 6
- lse: float32 [4, 16, 1024], P('dp', None, 'ctx'), may hold values from 3 to 5
- glob_keys: bfloat16 [128, 1024], replicated, may hold values from -6 to 6
- glob_values: bfloat16 [128, 1024], replicated, may hold values from -6 to 6
- rand_owner: int32 [16, 3], P('ctx'), may hold values from 0 to 7, all different within a row; in each aligned block of 2 rows (0 to 1, 2 to 3, ...) at most 2 rows name the same one
- rand_local: int32 [16, 3], P('ctx'), may hold values from 0 to 1
Outputs:
- d_queries: bfloat16 [4, 1024, 1024], P('dp', 'ctx')
- d_keys: bfloat16 [4, 1024, 1024], P('dp', 'ctx')
- d_values: bfloat16 [4, 1024, 1024], P('dp', 'ctx')
- d_glob_keys: float32 [128, 1024], replicated
- d_glob_values: float32 [128, 1024], replicated
Inputs may be any that keep to these rules, and one draw needn't show every extreme that they name: `rand_owner`: the 3 random blocks of one query block lie on different ctx indices. Among the 2 query blocks of one device no ctx index is named more than 2 times.
All inputs are finite; a program needn't handle non-finite values.
Results may differ from a plain program's by a relative error of at most 0.0055.
Values may be sent and summed in bfloat16 or wider, within the bound.
A program may use at most 128 MiB of HBM per device.

v0:
```python
import jax
import jax.numpy as jnp
from jax import lax
from jax.sharding import PartitionSpec as P

HEADS = 16
HDIM = 64
BLK = 64
GLOB = 128


def extended(block, sides, width):
    for axis, dim in sides:
        count = lax.axis_size(axis)
        forward = [(i, i + 1) for i in range(count - 1)]
        forward.append((count - 1, 0))
        backward = [(target, source) for source, target in forward]
        low = lax.ppermute(
            lax.slice_in_dim(block, block.shape[dim] - width, None, axis=dim), axis, forward
        )
        high = lax.ppermute(lax.slice_in_dim(block, 0, width, axis=dim), axis, backward)
        block = jnp.concatenate([low, block, high], axis=dim)
    return block


def block_grads(query_blk, dout_blk, lse_blk, delta_blk, key_blk, value_blk):
    scaling = HDIM ** (-0.5)
    scores = (
        jnp.einsum("nqhe,nkhe->nhqk", query_blk, key_blk, preferred_element_type=jnp.float32)
        * scaling
    )
    probability = jnp.exp(scores - lse_blk[..., None])
    prob_low = probability.astype(jnp.bfloat16)
    d_probability = jnp.einsum(
        "nqhe,nkhe->nhqk", dout_blk, value_blk, preferred_element_type=jnp.float32
    )
    d_scores = (probability * (d_probability - delta_blk[..., None])).astype(jnp.bfloat16)
    grad_q = (
        jnp.einsum("nhqk,nkhe->nqhe", d_scores, key_blk, preferred_element_type=jnp.float32)
        * scaling
    )
    grad_k = (
        jnp.einsum("nhqk,nqhe->nkhe", d_scores, query_blk, preferred_element_type=jnp.float32)
        * scaling
    )
    grad_v = jnp.einsum("nhqk,nqhe->nkhe", prob_low, dout_blk, preferred_element_type=jnp.float32)
    return (grad_q, grad_k, grad_v)


def spread_window(section):
    pad_rest = ((0, 0), (0, 0), (0, 0))
    lower = jnp.pad(section[:, :BLK], ((0, 2),) + pad_rest)
    middle = jnp.pad(section[:, BLK : 2 * BLK], ((1, 1),) + pad_rest)
    upper = jnp.pad(section[:, 2 * BLK :], ((2, 0),) + pad_rest)
    return lower + middle + upper


def shards(
    queries, keys, values, outputs, d_out, lse, glob_keys, glob_values, rand_owner, rand_local
):
    tokens_dev = queries.shape[1]
    feature_dim = queries.shape[2]
    blocks = tokens_dev // BLK
    cycle_size = lax.axis_size("ctx")
    per_block = rand_owner.shape[1]
    pairs = blocks * per_block
    query_blk = queries.reshape(blocks, BLK, HEADS, HDIM)
    dout_blk = d_out.reshape(blocks, BLK, HEADS, HDIM)
    product = d_out.astype(jnp.float32) * outputs.astype(jnp.float32)
    delta_blk = jnp.sum(product.reshape(blocks, BLK, HEADS, HDIM), axis=3).transpose(0, 2, 1)
    lse_blk = lse.reshape(HEADS, blocks, BLK).transpose(1, 0, 2)
    key_value = jnp.stack([keys[0], values[0]])
    padded = extended(key_value, (("ctx", 1),), BLK)

    def split_blocks(section):
        return section.reshape(2, blocks, BLK, HEADS, HDIM)

    window = jnp.concatenate(
        [
            split_blocks(padded[:, :tokens_dev]),
            split_blocks(padded[:, BLK : BLK + tokens_dev]),
            split_blocks(padded[:, 2 * BLK :]),
        ],
        axis=2,
    )
    dq_win, dk_win, dv_win = block_grads(
        query_blk, dout_blk, lse_blk, delta_blk, window[0], window[1]
    )
    grad_grid = jnp.stack([spread_window(dk_win), spread_window(dv_win)]).reshape(
        2, tokens_dev + 2 * BLK, feature_dim
    )
    edge_rims = jnp.concatenate([grad_grid[:, :BLK], grad_grid[:, tokens_dev + BLK :]], axis=1)
    returned = extended(edge_rims, (("ctx", 1),), BLK)
    kv_grad = grad_grid[:, BLK : tokens_dev + BLK]
    kv_grad = kv_grad.at[:, :BLK].add(returned[:, :BLK])
    kv_grad = kv_grad.at[:, tokens_dev - BLK :].add(returned[:, 3 * BLK :])
    mem_keys = jnp.broadcast_to(
        glob_keys.reshape(1, GLOB, HEADS, HDIM), (blocks, GLOB, HEADS, HDIM)
    )
    mem_values = jnp.broadcast_to(
        glob_values.reshape(1, GLOB, HEADS, HDIM), (blocks, GLOB, HEADS, HDIM)
    )
    dq_mem, dk_mem, dv_mem = block_grads(
        query_blk, dout_blk, lse_blk, delta_blk, mem_keys, mem_values
    )
    mem_terms = jnp.stack([jnp.sum(dk_mem, axis=0), jnp.sum(dv_mem, axis=0)]).reshape(
        2, GLOB, feature_dim
    )
    memory_total = lax.psum(mem_terms, ("dp", "ctx"))
    capacity = min(blocks, max(2, 2 * blocks * per_block // cycle_size))
    owner_flat = rand_owner.reshape(-1)
    local_flat = rand_local.reshape(-1)
    owner_hits = (owner_flat[:, None] == jnp.arange(cycle_size, dtype=jnp.int32)[None, :]).astype(
        jnp.int32
    )
    earlier = jnp.cumsum(owner_hits, axis=0) - owner_hits
    slot_rank = jnp.sum(earlier * owner_hits, axis=1)
    slot_index = owner_flat * capacity + slot_rank
    wanted = (
        jnp.zeros((cycle_size * capacity,), jnp.int32)
        .at[slot_index]
        .set(local_flat)
        .reshape(cycle_size, capacity)
    )
    kv_blocks = jnp.stack(
        [keys[0].reshape(blocks, BLK, feature_dim), values[0].reshape(blocks, BLK, feature_dim)],
        axis=1,
    )
    query_pairs = jnp.repeat(query_blk, per_block, axis=0)
    dout_pairs = jnp.repeat(dout_blk, per_block, axis=0)
    lse_pairs = jnp.repeat(lse_blk, per_block, axis=0)
    delta_pairs = jnp.repeat(delta_blk, per_block, axis=0)
    slots_all = cycle_size * capacity
    asked_ids = lax.all_to_all(wanted, "ctx", split_axis=0, concat_axis=0, tiled=True)
    picked = kv_blocks[asked_ids]
    fetched, asked_ids = (
        lax.all_to_all(picked, "ctx", split_axis=0, concat_axis=0, tiled=True),
        asked_ids,
    )
    chosen = fetched.reshape(slots_all, 2, BLK, HEADS, HDIM)[slot_index]
    dq_pair, dk_pair, dv_pair = block_grads(
        query_pairs, dout_pairs, lse_pairs, delta_pairs, chosen[:, 0], chosen[:, 1]
    )
    dq_rand = lax.optimization_barrier(dq_pair.astype(jnp.bfloat16)).astype(jnp.float32)
    pair_grads = (
        jnp.stack([dk_pair, dv_pair], axis=1)
        .reshape(pairs, 2, BLK, feature_dim)
        .astype(jnp.bfloat16)
    )
    grad_slots = (
        jnp.zeros((slots_all, 2, BLK, feature_dim), jnp.bfloat16).at[slot_index].set(pair_grads)
    )
    arrived = lax.all_to_all(
        grad_slots.reshape(cycle_size, capacity, 2, BLK, feature_dim),
        "ctx",
        split_axis=0,
        concat_axis=0,
        tiled=True,
    )
    received = arrived.reshape(slots_all, 2, BLK, feature_dim)
    kv_rand = (
        jnp.zeros((blocks, 2, BLK, feature_dim), jnp.float32)
        .at[asked_ids.reshape(-1)]
        .add(received.astype(jnp.float32))
    )
    dq_rand_sum = jnp.sum(dq_rand.reshape(blocks, per_block, BLK, HEADS, HDIM), axis=1)
    grad_queries = (
        (dq_win + dq_mem + dq_rand_sum).reshape(1, tokens_dev, feature_dim).astype(jnp.bfloat16)
    )
    grad_keys = (
        (kv_grad[0] + kv_rand[:, 0].reshape(tokens_dev, feature_dim))
        .reshape(1, tokens_dev, feature_dim)
        .astype(jnp.bfloat16)
    )
    grad_values = (
        (kv_grad[1] + kv_rand[:, 1].reshape(tokens_dev, feature_dim))
        .reshape(1, tokens_dev, feature_dim)
        .astype(jnp.bfloat16)
    )
    return (grad_queries, grad_keys, grad_values, memory_total[0], memory_total[1])


def solution(mesh):
    return jax.shard_map(
        shards,
        mesh=mesh,
        in_specs=(
            P("dp", "ctx", None),
            P("dp", "ctx", None),
            P("dp", "ctx", None),
            P("dp", "ctx", None),
            P("dp", "ctx", None),
            P("dp", None, "ctx"),
            P(),
            P(),
            P("ctx", None),
            P("ctx", None),
        ),
        out_specs=(P("dp", "ctx", None), P("dp", "ctx", None), P("dp", "ctx", None), P(), P()),
        check_vma=False,
    )
```

profile of v0, /device:TPU:0, one launch (start us, length us, event | category | flops | bytes accessed | tf_op | source)
XLA Modules:
  0.0 246.8 jit_solution(17565777443147992249)
XLA Ops:
  11.0 5.2 %all-to-all-start = ((s32[8,1,2]{2,1,0:T(1,128)}), s32[8,1,2]{2,1,0:T(1,128)S(1)}, u32[]{:S(2)}, u32[]{:S(2)}) async-start(s32[8,1,2]{2,1,0:T(1,128)} %bitcast.12), calls=%async_computation | async-start | bytes 8192 | tf_op jit(solution)/shard_map/all_to_all | solution.py:134
  17.3 3.5 %all-to-all-done = s32[8,1,2]{2,1,0:T(1,128)S(1)} async-done(((s32[8,1,2]{2,1,0:T(1,128)}), s32[8,1,2]{2,1,0:T(1,128)S(1)}, u32[]{:S(2)}, u32[]{:S(2)}) %all-to-all-start) | async-done | bytes 96 | tf_op jit(solution)/shard_map/all_to_all | solution.py:134
  21.0 2.8 %gather_fusion = bf16[16,2,64,1024]{3,2,1,0:T(8,128)(2,1)} fusion(bf16[2,2,64,1024]{3,2,0,1:T(8,128)(2,1)S(1)} %pad_maximum_fusion.5, s32[1024]{0:T(1024)S(1)} %pad_clamp_fusion.1), kind=kCustom, calls=%fused_computation | custom fusion | bytes 8388672 | tf_op jit(solution)/shard_map/gather | solution.py:135
  23.8 4.7 %all-to-all-start.1 = ((bf16[8,2,2,64,1024]{4,3,2,1,0:T(8,128)(2,1)}), bf16[8,2,2,64,1024]{4,3,2,1,0:T(8,128)(2,1)}, u32[]{:S(2)}, u32[]{:S(2)}) async-start(bf16[8,2,2,64,1024]{4,3,2,1,0:T(8,128)(2,1)} %bitcast.105), calls=%async_computation.1 | async-start | bytes 8388608 | tf_op jit(solution)/shard_map/all_to_all | solution.py:137
  29.9 2.3 collective-permute-start.1
  42.5 2.0 copy.129
  45.7 39.9 %collective-permute-done = bf16[2,64,1024]{2,1,0:T(8,128)(2,1)} collective-permute-done((bf16[2,64,1024]{2,1,0:T(8,128)(2,1)}, bf16[2,64,1024]{2,1,0:T(8,128)(2,1)}, u32[]{:S(2)}, u32[]{:S(2)}) %collective-permute-start) | collective-permute-done | bytes 262176 | tf_op jit(solution)/shard_map/ppermute | solution.py:18
  87.5 2.5 %reshape.256 = bf16[2,2,64,16,64]{4,3,2,1,0:T(8,128)(2,1)} reshape(bf16[2,128,1024]{2,1,0:T(8,128)(2,1)} %get-tuple-element.66) | data formatting | bytes 1048576 | tf_op jit(solution)/shard_map/reshape | solution.py:76
  90.0 2.7 %copy.130 = bf16[2,2,64,16,64]{2,4,3,1,0:T(8,128)(2,1)} copy(bf16[2,2,64,16,64]{4,3,2,1,0:T(8,128)(2,1)} %reshape.256) | data formatting | bytes 1048576 | tf_op jit(solution)/shard_map/reshape | solution.py:76
  94.3 2.7 %copy.128 = bf16[2,2,64,16,64]{2,4,3,1,0:T(8,128)(2,1)} copy(bf16[2,2,64,16,64]{4,3,2,1,0:T(8,128)(2,1)} %reshape.254) | data formatting | bytes 1048576 | tf_op jit(solution)/shard_map/reshape | solution.py:76
  97.0 2.5 %pad_maximum_fusion = bf16[2,2,192,16,64]{2,4,3,1,0:T(8,128)(2,1)S(1)} fusion(bf16[2,2,64,16,64]{2,4,3,1,0:T(8,128)(2,1)} %copy.130, bf16[2,2,64,16,64]{2,4,3,1,0:T(8,128)(2,1)S(1)} %copy.129, bf16[2,2,64,16,64]{2,4,3,1,0:T(8,128)(2,1)} %copy.128), kind=kLoop, calls=%fused_computation.12 | loop fusion | flops 4718592 | bytes 3145728 | tf_op jit(solution)/shard_map/concatenate | solution.py:78
  104.3 11.6 %reshape.262 = bf16[16,2,64,16,64]{4,3,2,1,0:T(8,128)(2,1)} reshape(bf16[8,2,2,64,1024]{4,3,2,1,0:T(8,128)(2,1)} %all-to-all-done.1) | data formatting | bytes 8388608 | tf_op jit(solution)/shard_map/reshape | solution.py:140
  115.9 4.5 %gather_fusion.1 = bf16[6,2,64,16,64]{4,3,2,1,0:T(8,128)(2,1)S(1)} fusion(bf16[16,2,64,16,64]{4,3,2,1,0:T(8,128)(2,1)} %reshape.262, s32[1024]{0:T(1024)S(1)} %pad_clamp_fusion), kind=kCustom, calls=%fused_computation.1 | custom fusion | bytes 3145752 | tf_op jit(solution)/shard_map/gather | solution.py:140
  125.7 2.2 copy.156
  127.9 3.4 %stack.39 = bf16[6,1,64,1024]{3,2,0,1:T(8,128)(2,1)} reshape(bf16[6,64,16,64]{3,2,1,0:T(8,128)(2,1)} %copy.156) | data formatting | bytes 1572864 | tf_op jit(solution)/shard_map/stack | solution.py:146
  131.4 3.1 %multiply_convert_fusion.2 = bf16[6,16,64,64]{3,2,1,0:T(8,128)(2,1)S(1)} fusion(f32[6,16,64,64]{3,2,1,0:T(8,128)S(1)} %fusion.10, bf16[6,64,16,64]{3,1,2,0:T(8,128)(2,1)} %bitcast.109, bf16[6,1,64,16,64]{4,3,2,1,0:T(8,128)(2,1)} %get-tuple-element.49, f32[6,16,64]{2,1,0:T(8,128)S(1)} %bitcast.127, f32[6,16,64]{2,1,0:T(8,128)S(1)} %bitcast.121), kind=kOutput, calls=%fused_computation.9 | convolution fusion | flops 52297728 | bytes 3981312 | tf_op jit(solution)/shard_map/nqhe,nkhe->nhqk/dot_general | solution.py:34
  138.1 2.5 %broadcast_in_dim.51 = bf16[16,2,64,1024]{3,2,1,0:T(8,128)(2,1)} broadcast(bf16[]{:T(256)} %constant.82.clone.1), dimensions={} | broadcast | bytes 4194306 | tf_op jit(solution)/shard_map/broadcast_in_dim | solution.py:151
  140.6 4.8 %scatter_fusion = bf16[16,2,64,1024]{3,2,1,0:T(8,128)(2,1)} fusion(bf16[16,2,64,1024]{3,2,1,0:T(8,128)(2,1)} %broadcast_in_dim.51, s32[6]{0:T(128)S(1)} %fusion.34, bf16[6,2,64,1024]{3,2,1,0:T(8,128)(2,1)S(1)} %copy.157), kind=kCustom, calls=%fused_computation.3 | custom fusion | bytes 4718616 | tf_op jit(solution)/shard_map/scatter | solution.py:151
  145.4 5.0 %all-to-all-start.2 = ((bf16[8,2,2,64,1024]{4,3,2,1,0:T(8,128)(2,1)}), bf16[8,2,2,64,1024]{4,3,2,1,0:T(8,128)(2,1)}, u32[]{:S(2)}, u32[]{:S(2)}) async-start(bf16[8,2,2,64,1024]{4,3,2,1,0:T(8,128)(2,1)} %bitcast.104), calls=%async_computation.2 | async-start | bytes 8388608 | tf_op jit(solution)/shard_map/all_to_all | solution.py:153
  151.2 2.0 copy.152
  153.3 2.9 %stack.35 = f32[1,256,1024]{2,1,0:T(8,128)} reshape(f32[4,64,16,64]{3,2,1,0:T(8,128)} %copy.152) | data formatting | bytes 2097152 | tf_op jit(solution)/shard_map/stack | solution.py:89
  158.1 2.0 copy.154
  160.1 2.1 stack.36
  164.8 2.5 collective-permute-start.3
  168.7 10.2 %all-reduce.8.cloned.1.call-done = f32[2,128,1024]{1,2,0:T(8,128)} async-done(((f32[2,128,1024]{1,2,0:T(8,128)}), f32[2,128,1024]{1,2,0:T(8,128)}) %all-reduce.8.cloned.1.call-update) | async-done | bytes 1048592 | tf_op jit(solution)/shard_map/psum | solution.py:109
  179.0 2.1 slice_bitcast_fusion.5
  182.0 2.2 copy.161
  184.2 27.9 %collective-permute-done.2 = f32[2,64,1024]{2,1,0:T(8,128)} collective-permute-done((f32[2,64,1024]{2,1,0:T(8,128)}, f32[2,64,1024]{2,1,0:T(8,128)}, u32[]{:S(2)}, u32[]{:S(2)}) %collective-permute-start.2) | collective-permute-done | bytes 524320 | tf_op jit(solution)/shard_map/ppermute | solution.py:18
  212.1 2.1 fusion.27
  214.2 2.1 fusion.26
  220.4 6.5 %bitcast_convert_fusion = f32[16,2,64,1024]{3,2,1,0:T(8,128)} fusion(bf16[8,2,2,64,1024]{4,3,2,1,0:T(8,128)(2,1)} %all-to-all-done.2), kind=kLoop, calls=%fused_computation.5 | loop fusion | flops 2097152 | bytes 12582912 | tf_op jit(solution)/shard_map/convert_element_type | solution.py:164
  227.0 10.7 %scatter_fusion.1 = f32[2,2,64,1024]{3,2,1,0:T(8,128)S(1)} fusion(f32[2,2,64,1024]{3,2,1,0:T(8,128)S(1)} %broadcast_in_dim.50, s32[16]{0:T(128)S(1)} %fusion.35, f32[16,2,64,1024]{3,2,1,0:T(8,128)} %bitcast_convert_fusion), kind=kCustom, calls=%fused_computation.4 | custom fusion | flops 2097152 | bytes 25165888 | tf_op jit(solution)/shard_map/scatter-add | solution.py:164
  (148 shorter events, 48.9 us)
Async XLA Ops:
  11.0 9.8 %all-to-all-start = ((s32[8,1,2]{2,1,0:T(1,128)}), s32[8,1,2]{2,1,0:T(1,128)S(1)}, u32[]{:S(2)}, u32[]{:S(2)}) async-start(s32[8,1,2]{2,1,0:T(1,128)} %bitcast.12), calls=%async_computation | async-start | bytes 8192 | tf_op jit(solution)/shard_map/all_to_all | solution.py:134
  23.8 4.8 %copy-start.26 = (bf16[1,128,1024]{2,1,0:T(8,128)(2,1)S(1)}, bf16[1,128,1024]{2,1,0:T(8,128)(2,1)}, u32[]{:S(2)}) copy-start(bf16[1,128,1024]{2,1,0:T(8,128)(2,1)} %param.15) | copy-start | bytes 786436
  23.8 4.9 %copy-start.27 = (bf16[1,128,1024]{2,1,0:T(8,128)(2,1)S(1)}, bf16[1,128,1024]{2,1,0:T(8,128)(2,1)}, u32[]{:S(2)}) copy-start(bf16[1,128,1024]{2,1,0:T(8,128)(2,1)} %param.16) | copy-start | bytes 786436
  23.8 80.5 %all-to-all-start.1 = ((bf16[8,2,2,64,1024]{4,3,2,1,0:T(8,128)(2,1)}), bf16[8,2,2,64,1024]{4,3,2,1,0:T(8,128)(2,1)}, u32[]{:S(2)}, u32[]{:S(2)}) async-start(bf16[8,2,2,64,1024]{4,3,2,1,0:T(8,128)(2,1)} %bitcast.105), calls=%async_computation.1 | async-start | bytes 8388608 | tf_op jit(solution)/shard_map/all_to_all | solution.py:137
  28.5 3.6 %copy-start.28 = (bf16[1,128,1024]{2,1,0:T(8,128)(2,1)S(1)}, bf16[1,128,1024]{2,1,0:T(8,128)(2,1)}, u32[]{:S(2)}) copy-start(bf16[1,128,1024]{2,1,0:T(8,128)(2,1)} %param.14) | copy-start | bytes 786436
  28.6 4.0 %copy-start.25 = (bf16[1,128,1024]{2,1,0:T(8,128)(2,1)S(1)}, bf16[1,128,1024]{2,1,0:T(8,128)(2,1)}, u32[]{:S(2)}) copy-start(bf16[1,128,1024]{2,1,0:T(8,128)(2,1)} %param.18) | copy-start | bytes 786436
  28.6 4.3 %copy-start.29 = (bf16[1,128,1024]{2,1,0:T(8,128)(2,1)S(1)}, bf16[1,128,1024]{2,1,0:T(8,128)(2,1)}, u32[]{:S(2)}) copy-start(bf16[1,128,1024]{2,1,0:T(8,128)(2,1)} %param.17) | copy-start | bytes 786436
  28.6 150.4 %all-reduce.8.cloned.1.call-start = ((), (), s32[]{:S(2)}) async-start(), calls=%async_computation.3 | async-start | bytes 2097152 | tf_op jit(solution)/shard_map/psum | solution.py:109
  29.5 56.1 %collective-permute-start = (bf16[2,64,1024]{2,1,0:T(8,128)(2,1)}, bf16[2,64,1024]{2,1,0:T(8,128)(2,1)}, u32[]{:S(2)}, u32[]{:S(2)}) collective-permute-start(bf16[2,64,1024]{2,1,0:T(8,128)(2,1)} %get-tuple-element.67), channel_id=1, source_target_pairs={{0,1},{1,2},{2,3},{3,4},{4,5},{5,6},{6,7},{7,0},{8,9},{9,10},{10,1... | collective-permute-start | bytes 786440 | tf_op jit(solution)/shard_map/ppermute | solution.py:18
  29.9 55.7 %collective-permute-start.1 = (bf16[2,64,1024]{2,1,0:T(8,128)(2,1)}, bf16[2,64,1024]{2,1,0:T(8,128)(2,1)}, u32[]{:S(2)}, u32[]{:S(2)}) collective-permute-start(bf16[2,64,1024]{2,1,0:T(8,128)(2,1)} %get-tuple-element.68), channel_id=1, source_target_pairs={{1,0},{2,1},{3,2},{4,3},{5,4},{6,5},{7,6},{0,7},{9,8},{10,9},{11,1... | collective-permute-start | bytes 786440 | tf_op jit(solution)/shard_map/ppermute | solution.py:21
  32.9 67.1 %copy-start.2 = (bf16[2,64,16,64]{3,2,1,0:T(8,128)(2,1)}, bf16[2,64,16,64]{3,2,1,0:T(8,128)(2,1)S(1)}, u32[]{:S(2)}) copy-start(bf16[2,64,16,64]{3,2,1,0:T(8,128)(2,1)S(1)} %reshape.259) | copy-start | bytes 786436
  99.6 1.3 copy-start.11
  100.0 1.5 copy-start
  120.5 1.8 copy-start.24
  122.3 1.4 copy-start.4
  122.7 1.3 copy-start.6
  122.7 1.4 copy-start.23
  131.4 3.1 %copy-start.7 = (bf16[2,3,64,16,64]{4,2,3,1,0:T(8,128)(2,1)S(1)}, bf16[2,3,64,16,64]{4,2,3,1,0:T(8,128)(2,1)}, u32[]{:S(2)}) copy-start(bf16[2,3,64,16,64]{4,2,3,1,0:T(8,128)(2,1)} %copy-done.6) | copy-start | bytes 2359300
  135.6 2.2 copy-start.22
  145.4 5.0 %copy-start.13 = (f32[2,192,16,64]{1,3,2,0:T(8,128)S(1)}, f32[2,192,16,64]{1,3,2,0:T(8,128)}, u32[]{:S(2)}) copy-start(f32[2,192,16,64]{1,3,2,0:T(8,128)} %multiply_bitcast_fusion) | copy-start | bytes 4718596
  145.4 75.0 %all-to-all-start.2 = ((bf16[8,2,2,64,1024]{4,3,2,1,0:T(8,128)(2,1)}), bf16[8,2,2,64,1024]{4,3,2,1,0:T(8,128)(2,1)}, u32[]{:S(2)}, u32[]{:S(2)}) async-start(bf16[8,2,2,64,1024]{4,3,2,1,0:T(8,128)(2,1)} %bitcast.104), calls=%async_computation.2 | async-start | bytes 8388608 | tf_op jit(solution)/shard_map/all_to_all | solution.py:153
  153.3 2.9 %copy-start.1 = (f32[2,16,192,64]{2,3,1,0:T(8,128)S(1)}, f32[2,16,192,64]{2,3,1,0:T(8,128)}, u32[]{:S(2)}) copy-start(f32[2,16,192,64]{2,3,1,0:T(8,128)} %copy-done) | copy-start | bytes 4718596
  153.3 2.9 %copy-start.3 = (bf16[2,64,16,64]{3,2,1,0:T(8,128)(2,1)S(1)}, bf16[2,64,16,64]{3,2,1,0:T(8,128)(2,1)}, u32[]{:S(2)}) copy-start(bf16[2,64,16,64]{3,2,1,0:T(8,128)(2,1)} %copy-done.2) | copy-start | bytes 786436
  160.1 2.1 copy-start.21
  162.4 2.2 copy-start.17
  162.4 4.9 %copy-start.12 = (bf16[2,2,192,16,64]{2,4,3,1,0:T(8,128)(2,1)S(1)}, bf16[2,2,192,16,64]{2,4,3,1,0:T(8,128)(2,1)}, u32[]{:S(2)}) copy-start(bf16[2,2,192,16,64]{2,4,3,1,0:T(8,128)(2,1)} %copy-done.11) | copy-start | bytes 4718596
  162.4 4.9 %copy-start.15 = (bf16[2,16,192,64]{2,3,1,0:T(8,128)(2,1)S(1)}, bf16[2,16,192,64]{2,3,1,0:T(8,128)(2,1)}, u32[]{:S(2)}) copy-start(bf16[2,16,192,64]{2,3,1,0:T(8,128)(2,1)} %copy-done.14) | copy-start | bytes 2359300
  164.6 47.5 %collective-permute-start.2 = (f32[2,64,1024]{2,1,0:T(8,128)}, f32[2,64,1024]{2,1,0:T(8,128)}, u32[]{:S(2)}, u32[]{:S(2)}) collective-permute-start(f32[2,64,1024]{2,1,0:T(8,128)} %get-tuple-element.52), channel_id=1, source_target_pairs={{0,1},{1,2},{2,3},{3,4},{4,5},{5,6},{6,7},{7,0},{8,9},{9,10},{10,1... | collective-permute-start | bytes 1572872 | tf_op jit(solution)/shard_map/ppermute | solution.py:18
  164.8 49.4 %collective-permute-start.3 = (f32[2,64,1024]{2,1,0:T(8,128)}, f32[2,64,1024]{2,1,0:T(8,128)}, u32[]{:S(2)}, u32[]{:S(2)}) collective-permute-start(f32[2,64,1024]{2,1,0:T(8,128)} %get-tuple-element.51), channel_id=1, source_target_pairs={{1,0},{2,1},{3,2},{4,3},{5,4},{6,5},{7,6},{0,7},{9,8},{10,9},{11,1... | collective-permute-start | bytes 1572872 | tf_op jit(solution)/shard_map/ppermute | solution.py:21
  182.0 34.3 %copy-start.5 = (bf16[6,1,64,16,64]{4,3,2,1,0:T(8,128)(2,1)S(1)}, bf16[6,1,64,16,64]{4,3,2,1,0:T(8,128)(2,1)}, u32[]{:S(2)}) copy-start(bf16[6,1,64,16,64]{4,3,2,1,0:T(8,128)(2,1)} %copy-done.4) | copy-start | bytes 2359300
  182.0 34.3 %copy-start.9 = (bf16[6,16,64,64]{3,2,1,0:T(8,128)(2,1)S(1)}, bf16[6,16,64,64]{3,2,1,0:T(8,128)(2,1)}, u32[]{:S(2)}) copy-start(bf16[6,16,64,64]{3,2,1,0:T(8,128)(2,1)} %copy-done.8) | copy-start | bytes 2359300
  217.1 1.4 copy-start.20
  (7 other events, 7.2 us)
Sparse Core Ops, SparseCore 0:
  39.0 139.8 all-reduce.7
where the time goes:
time: 248 us; the launch traced here: 247 us
  local copies, waits for them, and re-layouts  84.6 us (34%)
  waiting for transfers between devices  81.6 us (33%)
  other arithmetic  32.1 us (13%)
  starting transfers between devices  20.2 us (8%)
  between operations  14.7 us (6%)
  matrix products  13.6 us (5%)
    ppermute x2, waiting for transfers between devices, extended(): lax.ppermute(lax.slice_in_dim(block, block.shape[dim] - width, None, axis...  67.8 us
    reshape x6, local copies, waits for them, and re-layouts, split_blocks(): return section.reshape(2, blocks, BLK, HEADS, HDIM)  13.2 us
    reshape x1, local copies, waits for them, and re-layouts, shards(): chosen = fetched.reshape(slots_all, 2, BLK, HEADS, HDIM)[slot_index]  11.6 us
    unnamed x68, local copies, waits for them, and re-layouts  11.1 us
    scatter-add x1, other arithmetic, shards(): kv_rand = jnp.zeros((blocks, 2, BLK, feature_dim), jnp.float32).at[asked_...  10.7 us
    psum x1, waiting for transfers between devices, shards(): memory_total = lax.psum(mem_terms, ('dp', 'ctx'))  10.2 us
    convert_element_type x1, other arithmetic, shards(): received.astype(jnp.float32)  6.53 us
    all_to_all x1, starting transfers between devices, shards(): lax.all_to_all(wanted, 'ctx', split_axis=0, concat_axis=0, tiled=True)  5.17 us
  transfers between devices with their start and end apart: 8, of which 4 were waited for; matrix products, arithmetic and copies ran while one was open for 40% of the time, Pallas kernels for 0%

commit v1 on v0

v1 whole, which is shorter than its diff:
```python
import functools

import jax
import jax.numpy as jnp
from jax import lax
from jax.experimental import pallas as pl
from jax.experimental.pallas import tpu as pltpu
from jax.sharding import PartitionSpec as P

HEADS = 16
HDIM = 64
BLK = 64
GLOB = 128
NONE = -1e30
MESH = pl.DeviceIdType.MESH
F32 = jnp.float32
BF16 = jnp.bfloat16
NT = (((1,), (1,)), ((), ()))
NN = (((1,), (0,)), ((), ()))
Q, DO, SIDE, K, V, DK, DV, DQ, MEM = range(9)


def dot(a, b, dims):
    return lax.dot_general(a, b, dims, preferred_element_type=F32)


def kernel(
    n, n_dp, tokens, width, direct,
    owner_ref, local_ref, q_ref, k_ref, v_ref, o_ref, do_ref, lse_ref, gk_ref, gv_ref,
    dq_ref, dk_ref, dv_ref, dgk_ref, dgv_ref,
    q_all, do_all, k_all, v_all, side_out, side_all, dq_out, dk_out, dv_out, dq_sum,
    mem_out, mem_dp, tot_out, tot_all,
    send, recv, dp_send, dp_recv,
):
    me = lax.axis_index("ctx")
    me_dp = lax.axis_index("dp")
    heads = width // HDIM
    blocks = tokens // BLK
    total = n * blocks
    per_block = owner_ref.shape[1]
    scale = HDIM ** (-0.5)

    def peer(i):
        return lax.rem(me + i, n)

    def source(i):
        return lax.rem(me + n - i, n)

    def peer_dp(i):
        return lax.rem(me_dp + i, n_dp)

    def cols(ref, d):
        if direct:
            return ref.at[:, pl.ds(pl.multiple_of(d * width, width), width)]
        return ref.at[d]

    def rows(ref, d):
        return ref.at[pl.ds(pl.multiple_of(d * tokens, tokens), tokens), :]

    def lanes(ref, d):
        return ref.at[:, pl.ds(pl.multiple_of(d * tokens, tokens), tokens)]

    def remote(kind, src, dst, i, d):
        return pltpu.make_async_remote_copy(
            src_ref=src,
            dst_ref=dst,
            send_sem=send.at[kind, i],
            recv_sem=recv.at[kind, i],
            device_id={"ctx": d},
            device_id_type=MESH,
        )

    def incoming(kind, src_ref, all_ref, i):
        d = peer(i)
        return remote(kind, cols(src_ref, d), rows(all_ref, me), i, d)

    def side_copy(i):
        d = peer(i)
        return remote(SIDE, side_out.at[d], lanes(side_all, me), i, d)

    def outgoing(kind, out_ref, dst_ref, i):
        d = source(i)
        return remote(kind, rows(out_ref, d), cols(dst_ref, me), i, d)

    def dp_copy(i):
        return pltpu.make_async_remote_copy(
            src_ref=mem_out,
            dst_ref=mem_dp.at[i],
            send_sem=dp_send.at[i],
            recv_sem=dp_recv.at[i],
            device_id={"dp": peer_dp(i)},
            device_id_type=MESH,
        )

    def tot_copy(i):
        return remote(MEM, tot_out, tot_all.at[me], i, peer(i))

    barrier = pltpu.get_barrier_semaphore()
    for i in range(1, n):
        pl.semaphore_signal(barrier, inc=1, device_id={"ctx": peer(i)}, device_id_type=MESH)
    for i in range(1, n_dp):
        pl.semaphore_signal(barrier, inc=1, device_id={"dp": peer_dp(i)}, device_id_type=MESH)

    if direct:
        product = do_ref[...].astype(F32) * o_ref[...].astype(F32)
        head_of = lax.broadcasted_iota(jnp.int32, (HEADS, HEADS * HDIM), 1) // HDIM
        row_of = lax.broadcasted_iota(jnp.int32, (HEADS, HEADS * HDIM), 0)
        pick = jnp.where(head_of == row_of, 1.0, 0.0).astype(BF16)
        high = product.astype(BF16)
        low = (product - high.astype(F32)).astype(BF16)
        delta = dot(pick, high, NT) + dot(pick, low, NT)
    row = lax.broadcasted_iota(jnp.int32, (total, tokens), 0)
    lane_block = lax.broadcasted_iota(jnp.int32, (total, tokens), 1) // BLK
    count = jnp.zeros((total, tokens), F32)
    for b in range(blocks):
        g = me * blocks + b
        here = lane_block == b
        named = [lax.rem(g + total - 1, total), g, lax.rem(g + 1, total)]
        named += [owner_ref[b, r] * blocks + local_ref[b, r] for r in range(per_block)]
        for j in named:
            count = count + jnp.where(here & (row == j), 1.0, 0.0)
    bias = jnp.where(count > 0, jnp.log(jnp.maximum(count, 1.0)), NONE)
    for d in range(n):
        side_out[d, :total, :] = bias
        side_out[d, total : total + heads, :] = lse_ref[d * heads : (d + 1) * heads, :]
        if direct:
            part = delta[d * heads : (d + 1) * heads, :]
        else:
            product = do_ref[d].astype(F32) * o_ref[d].astype(F32)
            one = jnp.ones((8, width), BF16)
            high = product.astype(BF16)
            low = (product - high.astype(F32)).astype(BF16)
            part = (dot(one, high, NT) + dot(one, low, NT))[:heads]
        side_out[d, total + heads : total + 2 * heads, :] = part

    pl.semaphore_wait(barrier, n - 1 + n_dp - 1)

    for i in range(1, n):
        incoming(Q, q_ref, q_all, i).start()
        incoming(DO, do_ref, do_all, i).start()
        side_copy(i).start()
    for i in range(1, n):
        incoming(K, k_ref, k_all, i).start()
        incoming(V, v_ref, v_all, i).start()
    rows(q_all, me)[...] = cols(q_ref, me)[...]
    rows(do_all, me)[...] = cols(do_ref, me)[...]
    rows(k_all, me)[...] = cols(k_ref, me)[...]
    rows(v_all, me)[...] = cols(v_ref, me)[...]
    lanes(side_all, me)[...] = side_out[me]
    for i in range(1, n):
        incoming(Q, q_ref, q_all, i).wait_recv()
        incoming(DO, do_ref, do_all, i).wait_recv()
        side_copy(i).wait_recv()

    q_all[...] = (q_all[...].astype(F32) * scale).astype(BF16)
    lane_head = lax.broadcasted_iota(jnp.int32, (1, width), 1) // HDIM

    def stacked(block):
        if heads == 1:
            return block
        return jnp.concatenate(
            [jnp.where(lane_head == h, block, jnp.zeros_like(block)) for h in range(heads)], axis=0
        )

    def merged(full, size):
        out = full[:size]
        for h in range(1, heads):
            out = jnp.where(lane_head == h, full[h * size : (h + 1) * size], out)
        return out

    def grads(key_blk, value_blk, shift):
        size = key_blk.shape[0]
        key_st, value_st = stacked(key_blk), stacked(value_blk)
        queries, douts = q_all[...], do_all[...]
        scores = dot(key_st, queries, NT)
        d_prob = dot(value_st, douts, NT)
        prob_parts, ds_parts = [], []
        for h in range(heads):
            delta_row = side_all[total + heads + h : total + heads + h + 1, :]
            step = size // len(shift[h])
            for b, shift_row in enumerate(shift[h]):
                lo = h * size + b * step
                prob = jnp.exp(scores[lo : lo + step] - shift_row)
                prob_parts.append(prob.astype(BF16))
                ds_parts.append((prob * (d_prob[lo : lo + step] - delta_row)).astype(BF16))
        prob_low = jnp.concatenate(prob_parts, axis=0)
        d_scores = jnp.concatenate(ds_parts, axis=0)
        grad_q = dot(key_st.T, d_scores, NN)
        grad_k = merged(dot(d_scores, queries, NN), size)
        grad_v = merged(dot(prob_low, douts, NN), size)
        return grad_q, grad_k, grad_v

    def lse_row(h):
        return side_all[total + h : total + h + 1, :]

    grad_q, grad_k, grad_v = grads(
        cols(gk_ref, me)[...], cols(gv_ref, me)[...], [[lse_row(h)] for h in range(heads)]
    )
    dq_sum[...] = grad_q
    mem_out[0] = grad_k.astype(BF16)
    mem_out[1] = grad_v.astype(BF16)
    for i in range(1, n_dp):
        dp_copy(i).start()

    def step(i):
        s = source(i)
        shift = [
            [lse_row(h) - side_all[pl.ds(s * blocks + b, 1), :] for b in range(blocks)]
            for h in range(heads)
        ]
        grad_q, grad_k, grad_v = grads(rows(k_all, s)[...], rows(v_all, s)[...], shift)
        dq_sum[...] += grad_q
        return grad_k.astype(BF16), grad_v.astype(BF16)

    def far_step(i, carry):
        incoming(K, k_ref, k_all, i).wait_recv()
        incoming(V, v_ref, v_all, i).wait_recv()
        grad_k, grad_v = step(i)
        s = source(i)
        rows(dk_out, s)[...] = grad_k
        rows(dv_out, s)[...] = grad_v
        outgoing(DK, dk_out, dk_ref, i).start()
        outgoing(DV, dv_out, dv_ref, i).start()
        return carry

    grad_k, grad_v = step(0)
    cols(dk_ref, me)[...] = grad_k
    cols(dv_ref, me)[...] = grad_v

    for i in range(1, n_dp):
        dp_copy(i).wait_recv()
    summed = mem_out[...].astype(F32)
    for i in range(1, n_dp):
        summed = summed + mem_dp[i].astype(F32)
    tot_out[...] = summed.astype(BF16)
    for i in range(1, n):
        tot_copy(i).start()
    cols(dgk_ref, me)[...] = tot_out[0].astype(F32)
    cols(dgv_ref, me)[...] = tot_out[1].astype(F32)

    lax.fori_loop(1, n, far_step, 0)

    dq_out[...] = (dq_sum[...].T * scale).astype(BF16)
    for i in range(1, n):
        outgoing(DQ, dq_out, dq_ref, i).start()
    cols(dq_ref, me)[...] = rows(dq_out, me)[...]

    for i in range(1, n):
        tot_copy(i).wait_recv()
        s = source(i)
        cols(dgk_ref, s)[...] = tot_all[s, 0].astype(F32)
        cols(dgv_ref, s)[...] = tot_all[s, 1].astype(F32)
    for i in range(1, n):
        outgoing(DK, dk_out, dk_ref, i).wait_recv()
        outgoing(DV, dv_out, dv_ref, i).wait_recv()
        outgoing(DQ, dq_out, dq_ref, i).wait_recv()
    for i in range(1, n):
        incoming(Q, q_ref, q_all, i).wait_send()
        incoming(DO, do_ref, do_all, i).wait_send()
        side_copy(i).wait_send()
        incoming(K, k_ref, k_all, i).wait_send()
        incoming(V, v_ref, v_all, i).wait_send()
        outgoing(DK, dk_out, dk_ref, i).wait_send()
        outgoing(DV, dv_out, dv_ref, i).wait_send()
        outgoing(DQ, dq_out, dq_ref, i).wait_send()
        tot_copy(i).wait_send()
    for i in range(1, n_dp):
        dp_copy(i).wait_send()


def shards(
    queries, keys, values, outputs, d_out, lse, glob_keys, glob_values, rand_owner, rand_local
):
    n = lax.axis_size("ctx")
    n_dp = lax.axis_size("dp")
    tokens = queries.shape[1]
    features = queries.shape[2]
    width = features // n
    heads = width // HDIM
    direct = width % 128 == 0
    total = n * (tokens // BLK)
    side_rows = -(-(total + 2 * heads) // 8) * 8

    def split(x):
        if direct:
            return x
        return x.reshape(x.shape[0], n, width).transpose(1, 0, 2)

    def join(x):
        if direct:
            return x
        return x.transpose(1, 0, 2).reshape(x.shape[1], features)

    def like(count, dtype):
        shape = (count, features) if direct else (n, count, width)
        return jax.ShapeDtypeStruct(shape, dtype)

    vmem = pl.BlockSpec(memory_space=pltpu.VMEM)
    smem = pl.BlockSpec(memory_space=pltpu.SMEM)
    whole = pltpu.VMEM((n * tokens, width), BF16)
    results = pl.pallas_call(
        functools.partial(kernel, n, n_dp, tokens, width, direct),
        out_shape=[like(tokens, BF16)] * 3 + [like(GLOB, F32)] * 2,
        in_specs=[smem] * 2 + [vmem] * 8,
        out_specs=[vmem] * 5,
        scratch_shapes=[
            whole,
            whole,
            whole,
            whole,
            pltpu.VMEM((n, side_rows, tokens), F32),
            pltpu.VMEM((side_rows, n * tokens), F32),
            whole,
            whole,
            whole,
            pltpu.VMEM((width, n * tokens), F32),
            pltpu.VMEM((2, GLOB, width), BF16),
            pltpu.VMEM((n_dp, 2, GLOB, width), BF16),
            pltpu.VMEM((2, GLOB, width), BF16),
            pltpu.VMEM((n, 2, GLOB, width), BF16),
            pltpu.SemaphoreType.DMA((9, n)),
            pltpu.SemaphoreType.DMA((9, n)),
            pltpu.SemaphoreType.DMA((n_dp,)),
            pltpu.SemaphoreType.DMA((n_dp,)),
        ],
        compiler_params=pltpu.CompilerParams(
            collective_id=0, has_side_effects=True, vmem_limit_bytes=48 * 1024 * 1024
        ),
    )(
        rand_owner,
        rand_local,
        split(queries[0]),
        split(keys[0]),
        split(values[0]),
        split(outputs[0]),
        split(d_out[0]),
        lse[0],
        split(glob_keys),
        split(glob_values),
    )
    dq, dk, dv, dgk, dgv = [join(x) for x in results]
    return dq[None], dk[None], dv[None], dgk, dgv


def solution(mesh):
    return jax.shard_map(
        shards,
        mesh=mesh,
        in_specs=(
            P("dp", "ctx", None),
            P("dp", "ctx", None),
            P("dp", "ctx", None),
            P("dp", "ctx", None),
            P("dp", "ctx", None),
            P("dp", None, "ctx"),
            P(),
            P(),
            P("ctx", None),
            P("ctx", None),
        ),
        out_specs=(P("dp", "ctx", None), P("dp", "ctx", None), P("dp", "ctx", None), P(), P()),
        check_vma=False,
    )
```

time: 248 us -> 50.7 us (0.20)
  waiting for transfers between devices: 81.6 us -> 0 us
  local copies, waits for them, and re-layouts: 84.6 us -> 11 us
  Pallas kernels: 0 us -> 38.1 us
  other arithmetic: 32.1 us -> 0 us
  starting transfers between devices: 20.2 us -> 0 us
  between operations: 14.7 us -> 0.68 us
  matrix products: 13.6 us -> 0 us
    ppermute x4 -> x0, waiting for transfers between devices: 67.8 us -> none  [the longest x2 67.8 us: extended(): lax.ppermute(lax.slice_in_dim(block, block.shape[dim] - width, None, axis...]
    pallas_call x0 -> x1, Pallas kernels: none -> 38.1 us  [shards(): pl.pallas_call(functools.partial(kernel, n, n_dp, tokens, width, direct),...]
    reshape x16 -> x0, local copies, waits for them, and re-layouts: 28.5 us -> none  [the longest x6 13.2 us: split_blocks(): return section.reshape(2, blocks, BLK, HEADS, HDIM)]
    scatter-add x3 -> x0, other arithmetic: 14.9 us -> none  [the longest x1 10.7 us: shards(): kv_rand = jnp.zeros((blocks, 2, BLK, feature_dim), jnp.float32).at[asked_...]
    all_to_all x3 -> x0, starting transfers between devices: 14.9 us -> none  [the longest x1 5.17 us: shards(): lax.all_to_all(wanted, 'ctx', split_axis=0, concat_axis=0, tiled=True)]
    dot_general x15 -> x0, matrix products: 13.6 us -> none  [the longest x3 4.26 us: block_grads(): jnp.einsum('nqhe,nkhe->nhqk', dout_blk, value_blk, preferred_element_type...]
    psum x1 -> x0, waiting for transfers between devices: 10.2 us -> none  [shards(): memory_total = lax.psum(mem_terms, ('dp', 'ctx'))]
    another operation x7 -> x0, local copies, waits for them, and re-layouts: 9.88 us -> none  [the longest x3 5.1 us: shards(): jnp.stack([spread_window(dk_win), spread_window(dv_win)])]
  transfers between devices with their start and end apart: 8 -> 0, of which waited for: 4 -> 0; matrix products, arithmetic and copies ran while one was open for 40% -> 0% of each run, Pallas kernels for 0% -> 0%
where the time goes in v1:
time: 50.7 us; the launch traced here: 49.8 us
  Pallas kernels  38.1 us (75%)
  local copies, waits for them, and re-layouts  11 us (22%)
  between operations  0.68 us (1%)
    pallas_call x1, Pallas kernels, shards(): pl.pallas_call(functools.partial(kernel, n, n_dp, tokens, width, direct),...  38.1 us
    unnamed x25, local copies, waits for them, and re-layouts  11 us

profile of v1, /device:TPU:0, one launch (start us, length us, event | category | flops | bytes accessed | tf_op | source)
XLA Modules:
  0.0 49.8 jit_solution(7198413535127248993)
XLA Ops:
  0.6 0.0 copy-start.7
  0.6 0.0 copy-start.9
  0.7 0.0 copy-start.8
  0.7 0.7 %copy-done.7 = f32[1,16,128]{2,1,0:T(8,128)S(1)} copy-done((f32[1,16,128]{2,1,0:T(8,128)S(1)}, f32[1,16,128]{2,1,0:T(8,128)}, u32[]{:S(2)}) %copy-start.7) | copy-done | bytes 8216
  1.3 0.0 copy-done.9
  1.3 0.0 copy-done.8
  1.3 0.0 copy-start
  1.3 0.9 %copy-done = bf16[1,128,1024]{2,1,0:T(8,128)(2,1)S(1)} copy-done((bf16[1,128,1024]{2,1,0:T(8,128)(2,1)S(1)}, bf16[1,128,1024]{2,1,0:T(8,128)(2,1)}, u32[]{:S(2)}) %copy-start) | copy-done | bytes 262168
  2.3 0.0 copy-start.1
  2.3 0.9 %copy-done.1 = bf16[1,128,1024]{2,1,0:T(8,128)(2,1)S(1)} copy-done((bf16[1,128,1024]{2,1,0:T(8,128)(2,1)S(1)}, bf16[1,128,1024]{2,1,0:T(8,128)(2,1)}, u32[]{:S(2)}) %copy-start.1) | copy-done | bytes 262168
  3.2 0.0 copy-start.2
  3.2 0.9 %copy-done.2 = bf16[1,128,1024]{2,1,0:T(8,128)(2,1)S(1)} copy-done((bf16[1,128,1024]{2,1,0:T(8,128)(2,1)S(1)}, bf16[1,128,1024]{2,1,0:T(8,128)(2,1)}, u32[]{:S(2)}) %copy-start.2) | copy-done | bytes 262168
  4.2 0.0 copy-start.3
  4.2 0.9 %copy-done.3 = bf16[1,128,1024]{2,1,0:T(8,128)(2,1)S(1)} copy-done((bf16[1,128,1024]{2,1,0:T(8,128)(2,1)S(1)}, bf16[1,128,1024]{2,1,0:T(8,128)(2,1)}, u32[]{:S(2)}) %copy-start.3) | copy-done | bytes 262168
  5.1 0.0 copy-start.4
  5.2 0.9 %copy-done.4 = bf16[1,128,1024]{2,1,0:T(8,128)(2,1)S(1)} copy-done((bf16[1,128,1024]{2,1,0:T(8,128)(2,1)S(1)}, bf16[1,128,1024]{2,1,0:T(8,128)(2,1)}, u32[]{:S(2)}) %copy-start.4) | copy-done | bytes 262168
  6.1 0.0 copy-start.5
  6.1 0.9 %copy-done.5 = bf16[128,1024]{1,0:T(8,128)(2,1)S(1)} copy-done((bf16[128,1024]{1,0:T(8,128)(2,1)S(1)}, bf16[128,1024]{1,0:T(8,128)(2,1)}, u32[]{:S(2)}) %copy-start.5) | copy-done | bytes 262168
  7.0 0.0 copy-start.6
  7.1 0.9 %copy-done.6 = bf16[128,1024]{1,0:T(8,128)(2,1)S(1)} copy-done((bf16[128,1024]{1,0:T(8,128)(2,1)S(1)}, bf16[128,1024]{1,0:T(8,128)(2,1)}, u32[]{:S(2)}) %copy-start.6) | copy-done | bytes 262168
  8.0 38.1 %shard_map.137 = (bf16[128,1024]{1,0:T(8,128)(2,1)S(1)}, bf16[128,1024]{1,0:T(8,128)(2,1)S(1)}, bf16[128,1024]{1,0:T(8,128)(2,1)S(1)}, f32[128,1024]{1,0:T(8,128)S(1)}, f32[128,1024]{1,0:T(8,128)S(1)}) custom-call(s32[2,3]{1,0:T(2,128)S(1)} %copy-done.8, s32[2,3]{1,0:T(2,128)S(1)} %copy-done.9, bf16[128,1024]{1,0:T(8,128)(2,1)S(1)} %bitcast.12, ...), custom_call_target="tpu_custom_call" | custom-call | tf_op jit(solution)/shard_map/pallas_call | solution.py:301
  46.1 0.7 %copy.20 = bf16[1,128,1024]{2,1,0:T(8,128)(2,1)} copy(bf16[1,128,1024]{2,1,0:T(8,128)(2,1)S(1)} %bitcast.11) | data formatting | bytes 524288
  46.8 0.7 %copy.21 = bf16[1,128,1024]{2,1,0:T(8,128)(2,1)} copy(bf16[1,128,1024]{2,1,0:T(8,128)(2,1)S(1)} %bitcast.10) | data formatting | bytes 524288
  47.5 0.7 %copy.22 = bf16[1,128,1024]{2,1,0:T(8,128)(2,1)} copy(bf16[1,128,1024]{2,1,0:T(8,128)(2,1)S(1)} %bitcast.9) | data formatting | bytes 524288
  48.2 0.8 %copy.23 = f32[128,1024]{1,0:T(8,128)} copy(f32[128,1024]{1,0:T(8,128)S(1)} %get-tuple-element.23) | data formatting | bytes 1048576
  49.0 0.8 %copy.24 = f32[128,1024]{1,0:T(8,128)} copy(f32[128,1024]{1,0:T(8,128)S(1)} %get-tuple-element.24) | data formatting | bytes 1048576
Async XLA Ops:
  0.6 0.7 %copy-start.7 = (f32[1,16,128]{2,1,0:T(8,128)S(1)}, f32[1,16,128]{2,1,0:T(8,128)}, u32[]{:S(2)}) copy-start(f32[1,16,128]{2,1,0:T(8,128)} %param.15) | copy-start | bytes 24580
  0.6 0.7 %copy-start.9 = (s32[2,3]{1,0:T(2,128)S(1)}, s32[2,3]{1,0:T(2,128)}, u32[]{:S(2)}) copy-start(s32[2,3]{1,0:T(2,128)} %local_ref.1) | copy-start | bytes 76
  0.7 0.7 %copy-start.8 = (s32[2,3]{1,0:T(2,128)S(1)}, s32[2,3]{1,0:T(2,128)}, u32[]{:S(2)}) copy-start(s32[2,3]{1,0:T(2,128)} %owner_ref.1) | copy-start | bytes 76
  1.3 0.9 %copy-start = (bf16[1,128,1024]{2,1,0:T(8,128)(2,1)S(1)}, bf16[1,128,1024]{2,1,0:T(8,128)(2,1)}, u32[]{:S(2)}) copy-start(bf16[1,128,1024]{2,1,0:T(8,128)(2,1)} %param.10) | copy-start | bytes 786436
  2.3 0.9 %copy-start.1 = (bf16[1,128,1024]{2,1,0:T(8,128)(2,1)S(1)}, bf16[1,128,1024]{2,1,0:T(8,128)(2,1)}, u32[]{:S(2)}) copy-start(bf16[1,128,1024]{2,1,0:T(8,128)(2,1)} %param.11) | copy-start | bytes 786436
  3.2 0.9 %copy-start.2 = (bf16[1,128,1024]{2,1,0:T(8,128)(2,1)S(1)}, bf16[1,128,1024]{2,1,0:T(8,128)(2,1)}, u32[]{:S(2)}) copy-start(bf16[1,128,1024]{2,1,0:T(8,128)(2,1)} %param.12) | copy-start | bytes 786436
  4.2 0.9 %copy-start.3 = (bf16[1,128,1024]{2,1,0:T(8,128)(2,1)S(1)}, bf16[1,128,1024]{2,1,0:T(8,128)(2,1)}, u32[]{:S(2)}) copy-start(bf16[1,128,1024]{2,1,0:T(8,128)(2,1)} %param.13) | copy-start | bytes 786436
  5.1 0.9 %copy-start.4 = (bf16[1,128,1024]{2,1,0:T(8,128)(2,1)S(1)}, bf16[1,128,1024]{2,1,0:T(8,128)(2,1)}, u32[]{:S(2)}) copy-start(bf16[1,128,1024]{2,1,0:T(8,128)(2,1)} %param.14) | copy-start | bytes 786436
  6.1 0.9 %copy-start.5 = (bf16[128,1024]{1,0:T(8,128)(2,1)S(1)}, bf16[128,1024]{1,0:T(8,128)(2,1)}, u32[]{:S(2)}) copy-start(bf16[128,1024]{1,0:T(8,128)(2,1)} %gk_ref.1) | copy-start | bytes 786436
  7.0 0.9 %copy-start.6 = (bf16[128,1024]{1,0:T(8,128)(2,1)S(1)}, bf16[128,1024]{1,0:T(8,128)(2,1)}, u32[]{:S(2)}) copy-start(bf16[128,1024]{1,0:T(8,128)(2,1)} %gv_ref.1) | copy-start | bytes 786436

commit v2 on v1

--- a/solution.py
+++ b/solution.py
@@ -27,10 +27,10 @@
 def kernel(
     n, n_dp, tokens, width, direct,
     owner_ref, local_ref, q_ref, k_ref, v_ref, o_ref, do_ref, lse_ref, gk_ref, gv_ref,
-    dq_ref, dk_ref, dv_ref, dgk_ref, dgv_ref,
-    q_all, do_all, k_all, v_all, side_out, side_all, dq_out, dk_out, dv_out, dq_sum,
-    mem_out, mem_dp, tot_out, tot_all,
-    send, recv, dp_send, dp_recv,
+    dq_ref, dk_ref, dv_ref, tot_all,
+    o_vm, do_vm, lse_vm, gk_vm, gv_vm, q_all, do_all, k_all, v_all, side_out, side_all, dq_out, dk_out, dv_out, dq_sum,
+    mem_out, mem_dp, tot_out,
+    send, recv, dp_send, dp_recv, own,
 ):
     me = lax.axis_index("ctx")
     me_dp = lax.axis_index("dp")
@@ -101,8 +101,29 @@
     for i in range(1, n_dp):
         pl.semaphore_signal(barrier, inc=1, device_id={"dp": peer_dp(i)}, device_id_type=MESH)
 
+    loads = [
+        pltpu.make_async_copy(src, dst, own.at[i])
+        for i, (src, dst) in enumerate(
+            [
+                (o_ref, o_vm),
+                (do_ref, do_vm),
+                (lse_ref, lse_vm),
+                (cols(gk_ref, me), gk_vm),
+                (cols(gv_ref, me), gv_vm),
+                (cols(q_ref, me), rows(q_all, me)),
+                (cols(do_ref, me), rows(do_all, me)),
+                (cols(k_ref, me), rows(k_all, me)),
+                (cols(v_ref, me), rows(v_all, me)),
+            ]
+        )
+    ]
+    for load in loads:
+        load.start()
+    for load in loads[:3]:
+        load.wait()
+
     if direct:
-        product = do_ref[...].astype(F32) * o_ref[...].astype(F32)
+        product = do_vm[...].astype(F32) * o_vm[...].astype(F32)
         head_of = lax.broadcasted_iota(jnp.int32, (HEADS, HEADS * HDIM), 1) // HDIM
         row_of = lax.broadcasted_iota(jnp.int32, (HEADS, HEADS * HDIM), 0)
         pick = jnp.where(head_of == row_of, 1.0, 0.0).astype(BF16)
@@ -122,11 +143,11 @@
     bias = jnp.where(count > 0, jnp.log(jnp.maximum(count, 1.0)), NONE)
     for d in range(n):
         side_out[d, :total, :] = bias
-        side_out[d, total : total + heads, :] = lse_ref[d * heads : (d + 1) * heads, :]
+        side_out[d, total : total + heads, :] = lse_vm[d * heads : (d + 1) * heads, :]
         if direct:
             part = delta[d * heads : (d + 1) * heads, :]
         else:
-            product = do_ref[d].astype(F32) * o_ref[d].astype(F32)
+            product = do_vm[d].astype(F32) * o_vm[d].astype(F32)
             one = jnp.ones((8, width), BF16)
             high = product.astype(BF16)
             low = (product - high.astype(F32)).astype(BF16)
@@ -142,10 +163,8 @@
     for i in range(1, n):
         incoming(K, k_ref, k_all, i).start()
         incoming(V, v_ref, v_all, i).start()
-    rows(q_all, me)[...] = cols(q_ref, me)[...]
-    rows(do_all, me)[...] = cols(do_ref, me)[...]
-    rows(k_all, me)[...] = cols(k_ref, me)[...]
-    rows(v_all, me)[...] = cols(v_ref, me)[...]
+    for load in loads[3:]:
+        load.wait()
     lanes(side_all, me)[...] = side_out[me]
     for i in range(1, n):
         incoming(Q, q_ref, q_all, i).wait_recv()
@@ -194,7 +213,7 @@
         return side_all[total + h : total + h + 1, :]
 
     grad_q, grad_k, grad_v = grads(
-        cols(gk_ref, me)[...], cols(gv_ref, me)[...], [[lse_row(h)] for h in range(heads)]
+        gk_vm[...], gv_vm[...], [[lse_row(h)] for h in range(heads)]
     )
     dq_sum[...] = grad_q
     mem_out[0] = grad_k.astype(BF16)
@@ -233,10 +252,9 @@
     for i in range(1, n_dp):
         summed = summed + mem_dp[i].astype(F32)
     tot_out[...] = summed.astype(BF16)
+    tot_all[me] = tot_out[...]
     for i in range(1, n):
         tot_copy(i).start()
-    cols(dgk_ref, me)[...] = tot_out[0].astype(F32)
-    cols(dgv_ref, me)[...] = tot_out[1].astype(F32)
 
     lax.fori_loop(1, n, far_step, 0)
 
@@ -247,9 +265,6 @@
 
     for i in range(1, n):
         tot_copy(i).wait_recv()
-        s = source(i)
-        cols(dgk_ref, s)[...] = tot_all[s, 0].astype(F32)
-        cols(dgv_ref, s)[...] = tot_all[s, 1].astype(F32)
     for i in range(1, n):
         outgoing(DK, dk_out, dk_ref, i).wait_recv()
         outgoing(DV, dv_out, dv_ref, i).wait_recv()
@@ -266,6 +281,36 @@
         tot_copy(i).wait_send()
     for i in range(1, n_dp):
         dp_copy(i).wait_send()
+
+
+def finish(
+    n, width, direct, dq_ref, dk_ref, dv_ref, tot_ref,
+    dq_out, dk_out, dv_out, dgk_out, dgv_out, dgk_vm, dgv_vm, sem,
+):
+    copies = [
+        pltpu.make_async_copy(src, dst, sem.at[i])
+        for i, (src, dst) in enumerate(
+            [
+                (dq_ref, dq_out),
+                (dk_ref, dk_out),
+                (dv_ref, dv_out),
+                (dgk_vm, dgk_out),
+                (dgv_vm, dgv_out),
+            ]
+        )
+    ]
+    for copy in copies[:3]:
+        copy.start()
+    for part, (vm, copy) in enumerate(zip((dgk_vm, dgv_vm), copies[3:])):
+        for s in range(n):
+            value = tot_ref[s, part].astype(F32)
+            if direct:
+                vm[:, s * width : (s + 1) * width] = value
+            else:
+                vm[s] = value
+        copy.start()
+    for copy in copies:
+        copy.wait()
 
 
 def shards(
@@ -296,14 +341,21 @@
         return jax.ShapeDtypeStruct(shape, dtype)
 
     vmem = pl.BlockSpec(memory_space=pltpu.VMEM)
+    hbm = pl.BlockSpec(memory_space=pltpu.HBM)
     smem = pl.BlockSpec(memory_space=pltpu.SMEM)
     whole = pltpu.VMEM((n * tokens, width), BF16)
     results = pl.pallas_call(
         functools.partial(kernel, n, n_dp, tokens, width, direct),
-        out_shape=[like(tokens, BF16)] * 3 + [like(GLOB, F32)] * 2,
-        in_specs=[smem] * 2 + [vmem] * 8,
-        out_specs=[vmem] * 5,
+        out_shape=[like(tokens, BF16)] * 3
+        + [jax.ShapeDtypeStruct((n, 2, GLOB, width), BF16)],
+        in_specs=[smem] * 2 + [hbm] * 8,
+        out_specs=[vmem] * 4,
         scratch_shapes=[
+            pltpu.VMEM(like(tokens, BF16).shape, BF16),
+            pltpu.VMEM(like(tokens, BF16).shape, BF16),
+            pltpu.VMEM((HEADS, tokens), F32),
+            pltpu.VMEM((GLOB, width), BF16),
+            pltpu.VMEM((GLOB, width), BF16),
             whole,
             whole,
             whole,
@@ -317,14 +369,14 @@
             pltpu.VMEM((2, GLOB, width), BF16),
             pltpu.VMEM((n_dp, 2, GLOB, width), BF16),
             pltpu.VMEM((2, GLOB, width), BF16),
-            pltpu.VMEM((n, 2, GLOB, width), BF16),
             pltpu.SemaphoreType.DMA((9, n)),
             pltpu.SemaphoreType.DMA((9, n)),
             pltpu.SemaphoreType.DMA((n_dp,)),
             pltpu.SemaphoreType.DMA((n_dp,)),
+            pltpu.SemaphoreType.DMA((9,)),
         ],
         compiler_params=pltpu.CompilerParams(
-            collective_id=0, has_side_effects=True, vmem_limit_bytes=48 * 1024 * 1024
+            collective_id=0, has_side_effects=True, vmem_limit_bytes=63 * 1024 * 1024
         ),
     )(
         rand_owner,
@@ -338,6 +390,18 @@
         split(glob_keys),
         split(glob_values),
     )
+    results = pl.pallas_call(
+        functools.partial(finish, n, width, direct),
+        out_shape=[like(tokens, BF16)] * 3 + [like(GLOB, F32)] * 2,
+        in_specs=[hbm] * 3 + [vmem],
+        out_specs=[hbm] * 5,
+        scratch_shapes=[
+            pltpu.VMEM(like(GLOB, F32).shape, F32),
+            pltpu.VMEM(like(GLOB, F32).shape, F32),
+            pltpu.SemaphoreType.DMA((5,)),
+        ],
+        compiler_params=pltpu.CompilerParams(vmem_limit_bytes=63 * 1024 * 1024),
+    )(*results)
     dq, dk, dv, dgk, dgv = [join(x) for x in results]
     return dq[None], dk[None], dv[None], dgk, dgv
 

time: 50.7 us -> 67 us (1.32)
  Pallas kernels: 38.1 us -> 65.7 us
  local copies, waits for them, and re-layouts: 11 us -> 0 us
    pallas_call x0 -> x1, Pallas kernels: none -> 26 us  [shards(): pl.pallas_call(functools.partial(finish, n, width, direct), out_shape=[li...]
    unnamed x25 -> x0, local copies, waits for them, and re-layouts: 11 us -> none
    pallas_call x1, Pallas kernels: 38.1 us -> 39.7 us  [shards(): pl.pallas_call(functools.partial(kernel, n, n_dp, tokens, width, direct),...]
where the time goes in v2:
time: 67 us; the launch traced here: 66.3 us
  Pallas kernels  65.7 us (98%)
    pallas_call x1, Pallas kernels, shards(): pl.pallas_call(functools.partial(kernel, n, n_dp, tokens, width, direct),...  39.7 us
    pallas_call x1, Pallas kernels, shards(): pl.pallas_call(functools.partial(finish, n, width, direct), out_shape=[li...  26 us

profile of v2, /device:TPU:0, one launch (start us, length us, event | category | flops | bytes accessed | tf_op | source)
XLA Modules:
  0.0 66.3 jit_solution(6236392199976040730)
XLA Ops:
  0.6 39.7 %shard_map.137 = (bf16[128,1024]{1,0:T(8,128)(2,1)}, bf16[128,1024]{1,0:T(8,128)(2,1)}, bf16[128,1024]{1,0:T(8,128)(2,1)}, bf16[8,2,128,128]{3,2,1,0:T(8,128)(2,1)}) custom-call(s32[2,3]{1,0:T(2,128)} %owner_ref.1, s32[2,3]{1,0:T(2,128)} %local_ref.1, bf16[128,1024]{1,0:T(8,128)(2,1)} %bitcast.9, bf16[128,1024]{1,0:T(8,128)(2,1)} %bitcast.10, ...), custom_call_target="tpu_custom_call" | custom-call | tf_op jit(solution)/shard_map/pallas_call | solution.py:347
  40.3 26.0 %shard_map.138 = (bf16[128,1024]{1,0:T(8,128)(2,1)}, bf16[128,1024]{1,0:T(8,128)(2,1)}, bf16[128,1024]{1,0:T(8,128)(2,1)}, f32[128,1024]{1,0:T(8,128)}, f32[128,1024]{1,0:T(8,128)}) custom-call(bf16[128,1024]{1,0:T(8,128)(2,1)} %get-tuple-element.14.dq_ref, bf16[128,1024]{1,0:T(8,128)(2,1)} %get-tuple-element.15.dk_ref, ...), custom_call_target="tpu_custom_call" | custom-call | tf_op jit(solution)/shard_map/pallas_call | solution.py:393

commit v3 on v2

--- a/solution.py
+++ b/solution.py
@@ -17,7 +17,7 @@
 BF16 = jnp.bfloat16
 NT = (((1,), (1,)), ((), ()))
 NN = (((1,), (0,)), ((), ()))
-Q, DO, SIDE, K, V, DK, DV, DQ, MEM = range(9)
+Q, DO, SIDE, K, V, DK, DV, DQ, PART, CHIP, ALL_DP, CORE = range(12)
 
 
 def dot(a, b, dims):
@@ -29,8 +29,8 @@
     owner_ref, local_ref, q_ref, k_ref, v_ref, o_ref, do_ref, lse_ref, gk_ref, gv_ref,
     dq_ref, dk_ref, dv_ref, tot_all,
     o_vm, do_vm, lse_vm, gk_vm, gv_vm, q_all, do_all, k_all, v_all, side_out, side_all, dq_out, dk_out, dv_out, dq_sum,
-    mem_out, mem_dp, tot_out,
-    send, recv, dp_send, dp_recv, own,
+    mem_out, mem_dp,
+    send, recv, own,
 ):
     me = lax.axis_index("ctx")
     me_dp = lax.axis_index("dp")
@@ -82,18 +82,31 @@
         d = source(i)
         return remote(kind, rows(out_ref, d), cols(dst_ref, me), i, d)
 
-    def dp_copy(i):
+    core = lax.rem(me, 2)
+    quarter = GLOB // n_dp
+
+    def dp_remote(kind, src, dst, i):
         return pltpu.make_async_remote_copy(
-            src_ref=mem_out,
-            dst_ref=mem_dp.at[i],
-            send_sem=dp_send.at[i],
-            recv_sem=dp_recv.at[i],
+            src_ref=src,
+            dst_ref=dst,
+            send_sem=send.at[kind, i],
+            recv_sem=recv.at[kind, i],
             device_id={"dp": peer_dp(i)},
             device_id_type=MESH,
         )
 
-    def tot_copy(i):
-        return remote(MEM, tot_out, tot_all.at[me], i, peer(i))
+    def part_copy(i):
+        return dp_remote(PART, mem_out.at[peer_dp(i)], mem_dp.at[i], i)
+
+    def chip_copy(i):
+        block = tot_all.at[core, me_dp, me // 2]
+        return remote(CHIP, block, block, i, peer(2 * i))
+
+    def dp_copy(i):
+        return dp_remote(ALL_DP, tot_all.at[core, me_dp], tot_all.at[core, me_dp], i)
+
+    def core_copy():
+        return remote(CORE, tot_all.at[core], tot_all.at[core], 0, me + 1 - 2 * core)
 
     barrier = pltpu.get_barrier_semaphore()
     for i in range(1, n):
@@ -119,6 +132,10 @@
     ]
     for load in loads:
         load.start()
+    pl.semaphore_wait(barrier, n - 1 + n_dp - 1)
+    for i in range(1, n):
+        incoming(Q, q_ref, q_all, i).start()
+        incoming(DO, do_ref, do_all, i).start()
     for load in loads[:3]:
         load.wait()
 
@@ -154,11 +171,7 @@
             part = (dot(one, high, NT) + dot(one, low, NT))[:heads]
         side_out[d, total + heads : total + 2 * heads, :] = part
 
-    pl.semaphore_wait(barrier, n - 1 + n_dp - 1)
-
-    for i in range(1, n):
-        incoming(Q, q_ref, q_all, i).start()
-        incoming(DO, do_ref, do_all, i).start()
+    for i in range(1, n):
         side_copy(i).start()
     for i in range(1, n):
         incoming(K, k_ref, k_all, i).start()
@@ -216,10 +229,11 @@
         gk_vm[...], gv_vm[...], [[lse_row(h)] for h in range(heads)]
     )
     dq_sum[...] = grad_q
-    mem_out[0] = grad_k.astype(BF16)
-    mem_out[1] = grad_v.astype(BF16)
-    for i in range(1, n_dp):
-        dp_copy(i).start()
+    for p in range(n_dp):
+        mem_out[p, 0] = grad_k[p * quarter : (p + 1) * quarter].astype(BF16)
+        mem_out[p, 1] = grad_v[p * quarter : (p + 1) * quarter].astype(BF16)
+    for i in range(1, n_dp):
+        part_copy(i).start()
 
     def step(i):
         s = source(i)
@@ -234,6 +248,13 @@
     def far_step(i, carry):
         incoming(K, k_ref, k_all, i).wait_recv()
         incoming(V, v_ref, v_all, i).wait_recv()
+        @pl.when(i == 3)
+        def _():
+            for c in range(1, n // 2):
+                chip_copy(c).wait_recv()
+            for c in range(1, n_dp):
+                dp_copy(c).start()
+
         grad_k, grad_v = step(i)
         s = source(i)
         rows(dk_out, s)[...] = grad_k
@@ -247,14 +268,13 @@
     cols(dv_ref, me)[...] = grad_v
 
     for i in range(1, n_dp):
-        dp_copy(i).wait_recv()
-    summed = mem_out[...].astype(F32)
+        part_copy(i).wait_recv()
+    summed = mem_out[me_dp].astype(F32)
     for i in range(1, n_dp):
         summed = summed + mem_dp[i].astype(F32)
-    tot_out[...] = summed.astype(BF16)
-    tot_all[me] = tot_out[...]
-    for i in range(1, n):
-        tot_copy(i).start()
+    tot_all[core, me_dp, me // 2] = summed.astype(BF16)
+    for i in range(1, n // 2):
+        chip_copy(i).start()
 
     lax.fori_loop(1, n, far_step, 0)
 
@@ -263,8 +283,10 @@
         outgoing(DQ, dq_out, dq_ref, i).start()
     cols(dq_ref, me)[...] = rows(dq_out, me)[...]
 
-    for i in range(1, n):
-        tot_copy(i).wait_recv()
+    for i in range(1, n_dp):
+        dp_copy(i).wait_recv()
+    core_copy().start()
+    core_copy().wait_recv()
     for i in range(1, n):
         outgoing(DK, dk_out, dk_ref, i).wait_recv()
         outgoing(DV, dv_out, dv_ref, i).wait_recv()
@@ -278,15 +300,19 @@
         outgoing(DK, dk_out, dk_ref, i).wait_send()
         outgoing(DV, dv_out, dv_ref, i).wait_send()
         outgoing(DQ, dq_out, dq_ref, i).wait_send()
-        tot_copy(i).wait_send()
-    for i in range(1, n_dp):
+    for i in range(1, n_dp):
+        part_copy(i).wait_send()
         dp_copy(i).wait_send()
+    for i in range(1, n // 2):
+        chip_copy(i).wait_send()
+    core_copy().wait_send()
 
 
 def finish(
-    n, width, direct, dq_ref, dk_ref, dv_ref, tot_ref,
+    n, n_dp, width, direct, dq_ref, dk_ref, dv_ref, tot_ref,
     dq_out, dk_out, dv_out, dgk_out, dgv_out, dgk_vm, dgv_vm, sem,
 ):
+    quarter = GLOB // n_dp
     copies = [
         pltpu.make_async_copy(src, dst, sem.at[i])
         for i, (src, dst) in enumerate(
@@ -303,11 +329,13 @@
         copy.start()
     for part, (vm, copy) in enumerate(zip((dgk_vm, dgv_vm), copies[3:])):
         for s in range(n):
-            value = tot_ref[s, part].astype(F32)
-            if direct:
-                vm[:, s * width : (s + 1) * width] = value
-            else:
-                vm[s] = value
+            for p in range(n_dp):
+                value = tot_ref[s % 2, p, s // 2, part].astype(F32)
+                rows = slice(p * quarter, (p + 1) * quarter)
+                if direct:
+                    vm[rows, s * width : (s + 1) * width] = value
+                else:
+                    vm[s, rows] = value
         copy.start()
     for copy in copies:
         copy.wait()
@@ -346,8 +374,8 @@
     whole = pltpu.VMEM((n * tokens, width), BF16)
     results = pl.pallas_call(
         functools.partial(kernel, n, n_dp, tokens, width, direct),
-        out_shape=[like(tokens, BF16)] * 3
-        + [jax.ShapeDtypeStruct((n, 2, GLOB, width), BF16)],
+        out_shape=[pltpu.VMEM(like(tokens, BF16).shape, BF16)] * 3
+        + [pltpu.VMEM((2, n_dp, n // 2, 2, GLOB // n_dp, width), BF16)],
         in_specs=[smem] * 2 + [hbm] * 8,
         out_specs=[vmem] * 4,
         scratch_shapes=[
@@ -366,17 +394,14 @@
             whole,
             whole,
             pltpu.VMEM((width, n * tokens), F32),
-            pltpu.VMEM((2, GLOB, width), BF16),
-            pltpu.VMEM((n_dp, 2, GLOB, width), BF16),
-            pltpu.VMEM((2, GLOB, width), BF16),
-            pltpu.SemaphoreType.DMA((9, n)),
-            pltpu.SemaphoreType.DMA((9, n)),
-            pltpu.SemaphoreType.DMA((n_dp,)),
-            pltpu.SemaphoreType.DMA((n_dp,)),
+            pltpu.VMEM((n_dp, 2, GLOB // n_dp, width), BF16),
+            pltpu.VMEM((n_dp, 2, GLOB // n_dp, width), BF16),
+            pltpu.SemaphoreType.DMA((12, max(n, n_dp))),
+            pltpu.SemaphoreType.DMA((12, max(n, n_dp))),
             pltpu.SemaphoreType.DMA((9,)),
         ],
         compiler_params=pltpu.CompilerParams(
-            collective_id=0, has_side_effects=True, vmem_limit_bytes=63 * 1024 * 1024
+            collective_id=0, has_side_effects=True, vmem_limit_bytes=60 * 1024 * 1024
         ),
     )(
         rand_owner,
@@ -391,16 +416,16 @@
         split(glob_values),
     )
     results = pl.pallas_call(
-        functools.partial(finish, n, width, direct),
+        functools.partial(finish, n, n_dp, width, direct),
         out_shape=[like(tokens, BF16)] * 3 + [like(GLOB, F32)] * 2,
-        in_specs=[hbm] * 3 + [vmem],
+        in_specs=[vmem] * 4,
         out_specs=[hbm] * 5,
         scratch_shapes=[
             pltpu.VMEM(like(GLOB, F32).shape, F32),
             pltpu.VMEM(like(GLOB, F32).shape, F32),
             pltpu.SemaphoreType.DMA((5,)),
         ],
-        compiler_params=pltpu.CompilerParams(vmem_limit_bytes=63 * 1024 * 1024),
+        compiler_params=pltpu.CompilerParams(vmem_limit_bytes=16 * 1024 * 1024),
     )(*results)
     dq, dk, dv, dgk, dgv = [join(x) for x in results]
     return dq[None], dk[None], dv[None], dgk, dgv

time: 67 us -> 38.5 us (0.57)
  Pallas kernels: 65.7 us -> 37.7 us
    pallas_call x1, Pallas kernels: 26 us -> 1.27 us  [shards(): pl.pallas_call(functools.partial(finish, n, n_dp, width, direct), out_sha...]
    pallas_call x1, Pallas kernels: 39.7 us -> 36.4 us  [shards(): pl.pallas_call(functools.partial(kernel, n, n_dp, tokens, width, direct),...]
where the time goes in v3:
time: 38.5 us; the launch traced here: 38.3 us
  Pallas kernels  37.7 us (98%)
  between operations  0.64 us (2%)
    pallas_call x1, Pallas kernels, shards(): pl.pallas_call(functools.partial(kernel, n, n_dp, tokens, width, direct),...  36.4 us
    pallas_call x1, Pallas kernels, shards(): pl.pallas_call(functools.partial(finish, n, n_dp, width, direct), out_sha...  1.27 us

profile of v3, /device:TPU:0, one launch (start us, length us, event | category | flops | bytes accessed | tf_op | source)
XLA Modules:
  0.0 38.3 jit_solution(10238779285708573979)
XLA Ops:
  0.6 36.4 %shard_map.137 = (bf16[128,1024]{1,0:T(8,128)(2,1)S(1)}, bf16[128,1024]{1,0:T(8,128)(2,1)S(1)}, bf16[128,1024]{1,0:T(8,128)(2,1)S(1)}, bf16[2,4,4,2,32,128]{5,4,3,2,1,0:T(8,128)(2,1)S(1)}) custom-call(s32[2,3]{1,0:T(2,128)} %owner_ref.1, s32[2,3]{1,0:T(2,128)} %local_ref.1, bf16[128,1024]{1,0:T(8,128)(2,1)} %bitcast.9, bf16[128,1024]{1,0:T(8,128)(2,1)} %bitcast.10, ...), custom_call_target="tpu_custom_call" | custom-call | tf_op jit(solution)/shard_map/pallas_call | solution.py:375
  37.1 1.3 %shard_map.138 = (bf16[128,1024]{1,0:T(8,128)(2,1)}, bf16[128,1024]{1,0:T(8,128)(2,1)}, bf16[128,1024]{1,0:T(8,128)(2,1)}, f32[128,1024]{1,0:T(8,128)}, f32[128,1024]{1,0:T(8,128)}) custom-call(bf16[128,1024]{1,0:T(8,128)(2,1)S(1)} %get-tuple-element.14.dq_ref, bf16[128,1024]{1,0:T(8,128)(2,1)S(1)} %get-tuple-element.15.dk_ref, ...), custom_call_target="tpu_custom_call" | custom-call | tf_op jit(solution)/shard_map/pallas_call | solution.py:418

commit v4 on v3

--- a/solution.py
+++ b/solution.py
@@ -29,7 +29,7 @@
     owner_ref, local_ref, q_ref, k_ref, v_ref, o_ref, do_ref, lse_ref, gk_ref, gv_ref,
     dq_ref, dk_ref, dv_ref, tot_all,
     o_vm, do_vm, lse_vm, gk_vm, gv_vm, q_all, do_all, k_all, v_all, side_out, side_all, dq_out, dk_out, dv_out, dq_sum,
-    mem_out, mem_dp,
+    mem_out, mem_dp, named_by, bias,
     send, recv, own,
 ):
     me = lax.axis_index("ctx")
@@ -147,20 +147,18 @@
         high = product.astype(BF16)
         low = (product - high.astype(F32)).astype(BF16)
         delta = dot(pick, high, NT) + dot(pick, low, NT)
-    row = lax.broadcasted_iota(jnp.int32, (total, tokens), 0)
-    lane_block = lax.broadcasted_iota(jnp.int32, (total, tokens), 1) // BLK
-    count = jnp.zeros((total, tokens), F32)
+    lane = lax.broadcasted_iota(jnp.int32, (1, tokens), 1)
+    counts = []
     for b in range(blocks):
         g = me * blocks + b
-        here = lane_block == b
         named = [lax.rem(g + total - 1, total), g, lax.rem(g + 1, total)]
         named += [owner_ref[b, r] * blocks + local_ref[b, r] for r in range(per_block)]
+        count = jnp.zeros((1, tokens), F32)
         for j in named:
-            count = count + jnp.where(here & (row == j), 1.0, 0.0)
-    bias = jnp.where(count > 0, jnp.log(jnp.maximum(count, 1.0)), NONE)
+            count = count + jnp.where(lane == j, 1.0, 0.0)
+        counts.append(count)
     for d in range(n):
-        side_out[d, :total, :] = bias
-        side_out[d, total : total + heads, :] = lse_vm[d * heads : (d + 1) * heads, :]
+        side_out[d, :heads, :] = lse_vm[d * heads : (d + 1) * heads, :]
         if direct:
             part = delta[d * heads : (d + 1) * heads, :]
         else:
@@ -169,10 +167,15 @@
             high = product.astype(BF16)
             low = (product - high.astype(F32)).astype(BF16)
             part = (dot(one, high, NT) + dot(one, low, NT))[:heads]
-        side_out[d, total + heads : total + 2 * heads, :] = part
+        side_out[d, heads : 2 * heads, :] = part
+        for b in range(blocks):
+            side_out[d, 2 * heads + b : 2 * heads + b + 1, :] = counts[b]
 
     for i in range(1, n):
         side_copy(i).start()
+    for i in range(1, n):
+        incoming(Q, q_ref, q_all, i).wait_send()
+        incoming(DO, do_ref, do_all, i).wait_send()
     for i in range(1, n):
         incoming(K, k_ref, k_all, i).start()
         incoming(V, v_ref, v_all, i).start()
@@ -208,7 +211,7 @@
         d_prob = dot(value_st, douts, NT)
         prob_parts, ds_parts = [], []
         for h in range(heads):
-            delta_row = side_all[total + heads + h : total + heads + h + 1, :]
+            delta_row = side_all[heads + h : heads + h + 1, :]
             step = size // len(shift[h])
             for b, shift_row in enumerate(shift[h]):
                 lo = h * size + b * step
@@ -223,7 +226,7 @@
         return grad_q, grad_k, grad_v
 
     def lse_row(h):
-        return side_all[total + h : total + h + 1, :]
+        return side_all[h : h + 1, :]
 
     grad_q, grad_k, grad_v = grads(
         gk_vm[...], gv_vm[...], [[lse_row(h)] for h in range(heads)]
@@ -235,10 +238,21 @@
     for i in range(1, n_dp):
         part_copy(i).start()
 
+    for d in range(n):
+        for b in range(blocks):
+            named_by[d * blocks + b : d * blocks + b + 1, :] = side_all[
+                2 * heads + b : 2 * heads + b + 1, d * tokens : (d + 1) * tokens
+            ]
+    block_of = lax.broadcasted_iota(jnp.int32, (total, n * tokens), 1) // BLK
+    row_of = lax.broadcasted_iota(jnp.int32, (total, n * tokens), 0)
+    spread = jnp.where(block_of == row_of, 1.0, 0.0).astype(BF16)
+    count = dot(named_by[...].T.astype(BF16), spread, NN)[:total]
+    bias[...] = jnp.where(count > 0, jnp.log(jnp.maximum(count, 1.0)), NONE)
+
     def step(i):
         s = source(i)
         shift = [
-            [lse_row(h) - side_all[pl.ds(s * blocks + b, 1), :] for b in range(blocks)]
+            [lse_row(h) - bias[pl.ds(s * blocks + b, 1), :] for b in range(blocks)]
             for h in range(heads)
         ]
         grad_q, grad_k, grad_v = grads(rows(k_all, s)[...], rows(v_all, s)[...], shift)
@@ -248,7 +262,18 @@
     def far_step(i, carry):
         incoming(K, k_ref, k_all, i).wait_recv()
         incoming(V, v_ref, v_all, i).wait_recv()
-        @pl.when(i == 3)
+        @pl.when(i == 2)
+        def _():
+            for c in range(1, n_dp):
+                part_copy(c).wait_recv()
+            summed = mem_out[me_dp].astype(F32)
+            for c in range(1, n_dp):
+                summed = summed + mem_dp[c].astype(F32)
+            tot_all[core, me_dp, me // 2] = summed.astype(BF16)
+            for c in range(1, n // 2):
+                chip_copy(c).start()
+
+        @pl.when(i == 5)
         def _():
             for c in range(1, n // 2):
                 chip_copy(c).wait_recv()
@@ -267,15 +292,6 @@
     cols(dk_ref, me)[...] = grad_k
     cols(dv_ref, me)[...] = grad_v
 
-    for i in range(1, n_dp):
-        part_copy(i).wait_recv()
-    summed = mem_out[me_dp].astype(F32)
-    for i in range(1, n_dp):
-        summed = summed + mem_dp[i].astype(F32)
-    tot_all[core, me_dp, me // 2] = summed.astype(BF16)
-    for i in range(1, n // 2):
-        chip_copy(i).start()
-
     lax.fori_loop(1, n, far_step, 0)
 
     dq_out[...] = (dq_sum[...].T * scale).astype(BF16)
@@ -292,8 +308,6 @@
         outgoing(DV, dv_out, dv_ref, i).wait_recv()
         outgoing(DQ, dq_out, dq_ref, i).wait_recv()
     for i in range(1, n):
-        incoming(Q, q_ref, q_all, i).wait_send()
-        incoming(DO, do_ref, do_all, i).wait_send()
         side_copy(i).wait_send()
         incoming(K, k_ref, k_all, i).wait_send()
         incoming(V, v_ref, v_all, i).wait_send()
@@ -352,7 +366,7 @@
     heads = width // HDIM
     direct = width % 128 == 0
     total = n * (tokens // BLK)
-    side_rows = -(-(total + 2 * heads) // 8) * 8
+    side_rows = -(-(2 * heads + tokens // BLK) // 8) * 8
 
     def split(x):
         if direct:
@@ -396,6 +410,8 @@
             pltpu.VMEM((width, n * tokens), F32),
             pltpu.VMEM((n_dp, 2, GLOB // n_dp, width), BF16),
             pltpu.VMEM((n_dp, 2, GLOB // n_dp, width), BF16),
+            pltpu.VMEM((total, tokens), F32),
+            pltpu.VMEM((total, n * tokens), F32),
             pltpu.SemaphoreType.DMA((12, max(n, n_dp))),
             pltpu.SemaphoreType.DMA((12, max(n, n_dp))),
             pltpu.SemaphoreType.DMA((9,)),

time: 38.5 us -> 35.6 us (0.925)
  Pallas kernels: 37.7 us -> 34.8 us
    pallas_call x1, Pallas kernels: 36.4 us -> 33.5 us  [shards(): pl.pallas_call(functools.partial(kernel, n, n_dp, tokens, width, direct),...]
where the time goes in v4:
time: 35.6 us; the launch traced here: 35.4 us
  Pallas kernels  34.8 us (98%)
  between operations  0.64 us (2%)
    pallas_call x1, Pallas kernels, shards(): pl.pallas_call(functools.partial(kernel, n, n_dp, tokens, width, direct),...  33.5 us
    pallas_call x1, Pallas kernels, shards(): pl.pallas_call(functools.partial(finish, n, n_dp, width, direct), out_sha...  1.27 us

profile of v4, /device:TPU:0, one launch (start us, length us, event | category | flops | bytes accessed | tf_op | source)
XLA Modules:
  0.0 35.4 jit_solution(4544358853099893457)
XLA Ops:
  0.6 33.5 %shard_map.137 = (bf16[128,1024]{1,0:T(8,128)(2,1)S(1)}, bf16[128,1024]{1,0:T(8,128)(2,1)S(1)}, bf16[128,1024]{1,0:T(8,128)(2,1)S(1)}, bf16[2,4,4,2,32,128]{5,4,3,2,1,0:T(8,128)(2,1)S(1)}) custom-call(s32[2,3]{1,0:T(2,128)} %owner_ref.1, s32[2,3]{1,0:T(2,128)} %local_ref.1, bf16[128,1024]{1,0:T(8,128)(2,1)} %bitcast.9, bf16[128,1024]{1,0:T(8,128)(2,1)} %bitcast.10, ...), custom_call_target="tpu_custom_call" | custom-call | tf_op jit(solution)/shard_map/pallas_call | solution.py:389
  34.1 1.3 %shard_map.138 = (bf16[128,1024]{1,0:T(8,128)(2,1)}, bf16[128,1024]{1,0:T(8,128)(2,1)}, bf16[128,1024]{1,0:T(8,128)(2,1)}, f32[128,1024]{1,0:T(8,128)}, f32[128,1024]{1,0:T(8,128)}) custom-call(bf16[128,1024]{1,0:T(8,128)(2,1)S(1)} %get-tuple-element.14.dq_ref, bf16[128,1024]{1,0:T(8,128)(2,1)S(1)} %get-tuple-element.15.dk_ref, ...), custom_call_target="tpu_custom_call" | custom-call | tf_op jit(solution)/shard_map/pallas_call | solution.py:434

commit v5 on v4

--- a/solution.py
+++ b/solution.py
@@ -105,8 +105,9 @@
     def dp_copy(i):
         return dp_remote(ALL_DP, tot_all.at[core, me_dp], tot_all.at[core, me_dp], i)
 
-    def core_copy():
-        return remote(CORE, tot_all.at[core], tot_all.at[core], 0, me + 1 - 2 * core)
+    def core_copy(i):
+        block = tot_all.at[core, lax.rem(me_dp + n_dp - i, n_dp)]
+        return remote(CORE, block, block, i, me + 1 - 2 * core)
 
     barrier = pltpu.get_barrier_semaphore()
     for i in range(1, n):
@@ -279,6 +280,7 @@
                 chip_copy(c).wait_recv()
             for c in range(1, n_dp):
                 dp_copy(c).start()
+            core_copy(0).start()
 
         grad_k, grad_v = step(i)
         s = source(i)
@@ -301,8 +303,9 @@
 
     for i in range(1, n_dp):
         dp_copy(i).wait_recv()
-    core_copy().start()
-    core_copy().wait_recv()
+        core_copy(i).start()
+    for i in range(n_dp):
+        core_copy(i).wait_recv()
     for i in range(1, n):
         outgoing(DK, dk_out, dk_ref, i).wait_recv()
         outgoing(DV, dv_out, dv_ref, i).wait_recv()
@@ -319,7 +322,8 @@
         dp_copy(i).wait_send()
     for i in range(1, n // 2):
         chip_copy(i).wait_send()
-    core_copy().wait_send()
+    for i in range(n_dp):
+        core_copy(i).wait_send()
 
 
 def finish(

time: 35.6 us -> 35.6 us (level)
  no operation moved by 1% of the time
where the time goes in v5:
time: 35.6 us; the launch traced here: 35.5 us
  Pallas kernels  34.8 us (98%)
  between operations  0.64 us (2%)
    pallas_call x1, Pallas kernels, shards(): pl.pallas_call(functools.partial(kernel, n, n_dp, tokens, width, direct),...  33.5 us
    pallas_call x1, Pallas kernels, shards(): pl.pallas_call(functools.partial(finish, n, n_dp, width, direct), out_sha...  1.27 us

profile of v5, /device:TPU:0, one launch (start us, length us, event | category | flops | bytes accessed | tf_op | source)
XLA Modules:
  0.0 35.5 jit_solution(7083001766475390854)
XLA Ops:
  0.6 33.5 %shard_map.137 = (bf16[128,1024]{1,0:T(8,128)(2,1)S(1)}, bf16[128,1024]{1,0:T(8,128)(2,1)S(1)}, bf16[128,1024]{1,0:T(8,128)(2,1)S(1)}, bf16[2,4,4,2,32,128]{5,4,3,2,1,0:T(8,128)(2,1)S(1)}) custom-call(s32[2,3]{1,0:T(2,128)} %owner_ref.1, s32[2,3]{1,0:T(2,128)} %local_ref.1, bf16[128,1024]{1,0:T(8,128)(2,1)} %bitcast.9, bf16[128,1024]{1,0:T(8,128)(2,1)} %bitcast.10, ...), custom_call_target="tpu_custom_call" | custom-call | tf_op jit(solution)/shard_map/pallas_call | solution.py:393
  34.2 1.3 %shard_map.138 = (bf16[128,1024]{1,0:T(8,128)(2,1)}, bf16[128,1024]{1,0:T(8,128)(2,1)}, bf16[128,1024]{1,0:T(8,128)(2,1)}, f32[128,1024]{1,0:T(8,128)}, f32[128,1024]{1,0:T(8,128)}) custom-call(bf16[128,1024]{1,0:T(8,128)(2,1)S(1)} %get-tuple-element.14.dq_ref, bf16[128,1024]{1,0:T(8,128)(2,1)S(1)} %get-tuple-element.15.dk_ref, ...), custom_call_target="tpu_custom_call" | custom-call | tf_op jit(solution)/shard_map/pallas_call | solution.py:438
